TPU v7x, 256 devices: a whole 4x4x8 slice. The times are simulated.
256 devices in a mesh: grp: 8 (over x, y_lo), wide: 32 (over y_hi, z, core).
Axes of the slice: x: 4, y: 4 (y_hi: 2, y_lo: 2; y = y_hi * 2 + y_lo), z: 8, core: 2. Of those that a mesh axis runs over, the one named last changes fastest.
Arguments:
- src_rows: float32 [262144, 400], P(('grp', 'wide')), may hold values from -16 to 16
- src_accum: float32 [262144], P(('grp', 'wide')), may hold values from 0.1 to 4
- dst_rows: float32 [16384, 400], P(('grp', 'wide')), may hold values from -1.5 to 1.5
- dst_accum: float32 [16384], P(('grp', 'wide')), may hold values from 0.1 to 4
- relations: float32 [1024, 400], replicated, may hold values from -4 to 4
- rel_ids: int32 [2, 262144], P(None, ('grp', 'wide')), may hold values from 0 to 1023
- targets: int32 [2, 262144], P(None, ('grp', 'wide')), may hold values from 0 to 2047
Outputs:
- new_src: float32 [262144, 400], P(('grp', 'wide'))
- new_src_accum: float32 [262144], P(('grp', 'wide'))
- new_dst: float32 [16384, 400], P(('grp', 'wide'))
- new_dst_accum: float32 [16384], P(('grp', 'wide'))
- edge_loss: float32 [2, 262144], P(None, ('grp', 'wide'))
All inputs are finite; a program needn't handle non-finite values.
Results may differ from a plain program's by a relative error of at most 0.009.
Values may be sent and summed in bfloat16 or wider, within the bound.
A program may use at most 64 MiB of HBM per device.

v0:
```python
import jax
import jax.numpy as jnp
from jax import lax
from jax.sharding import PartitionSpec as P

ROUNDS = 2


LEARN_RATE = 0.1


def passed_along(block, axis, distance):
    devices = range(lax.axis_size(axis))
    route = [((i - distance) % len(devices), i) for i in devices]
    return lax.ppermute(block, axis, route)


def adagrad(table_rows, accumulator, gradients):
    accumulator = accumulator + jnp.mean(gradients * gradients, axis=-1)
    return (table_rows - LEARN_RATE * gradients / jnp.sqrt(accumulator)[..., None], accumulator)


def score_blocks(key_rows, query_rows, label_ids):
    src_count, feat_width = query_rows.shape
    block_rows = 512
    block_count = src_count // block_rows

    def visit(running, pieces):
        query, labels = pieces
        logits = jnp.einsum("sd,bd->sb", query, key_rows, preferred_element_type=jnp.float32)
        top_score = jnp.max(logits, axis=1, keepdims=True)
        exp_scores = jnp.exp(logits - top_score)
        exp_total = jnp.sum(exp_scores, axis=1, keepdims=True)
        target_hit = lax.broadcasted_iota(jnp.int32, logits.shape, 1) == labels[:, None]
        picked = jnp.sum(jnp.where(target_hit, logits, 0.0), axis=1)
        losses = top_score[:, 0] + jnp.log(exp_total[:, 0]) - picked
        residual = (exp_scores / exp_total - target_hit.astype(jnp.float32)).astype(jnp.bfloat16)
        grad_query = jnp.dot(residual, key_rows, preferred_element_type=jnp.float32)
        running = running + jnp.einsum(
            "sb,sd->bd", residual, query, preferred_element_type=jnp.float32
        )
        return (running, (losses, grad_query))

    pieces = (
        query_rows.reshape(block_count, block_rows, feat_width),
        label_ids.reshape(block_count, block_rows),
    )
    zeros = jnp.zeros((key_rows.shape[0], feat_width), jnp.float32)
    running, outputs = lax.scan(visit, zeros, pieces)
    losses, grad_query = outputs
    return (losses.reshape(src_count), grad_query.reshape(src_count, feat_width), running)


def shards(src_rows, src_accum, dst_rows, dst_accum, relations, rel_ids, targets):
    loss_list = []
    for round_index in range(ROUNDS):
        key_rows = lax.all_gather(dst_rows.astype(jnp.bfloat16), "wide", axis=0, tiled=True)
        rel_scales = jnp.take(relations, rel_ids[round_index], axis=0)
        query_rows = (src_rows * rel_scales).astype(jnp.bfloat16)
        label_ids = targets[round_index]
        losses, grad_query, partial_value = score_blocks(key_rows, query_rows, label_ids)
        grad_dst = lax.psum_scatter(
            partial_value.astype(jnp.bfloat16), "wide", scatter_dimension=0, tiled=True
        ).astype(jnp.float32)
        src_rows, src_accum = adagrad(src_rows, src_accum, grad_query * rel_scales)
        dst_rows, dst_accum = adagrad(dst_rows, dst_accum, grad_dst)
        loss_list.append(losses)
        if round_index + 1 < ROUNDS:
            dst_rows, dst_accum = passed_along((dst_rows, dst_accum), "grp", 1)
    return (src_rows, src_accum, dst_rows, dst_accum, jnp.stack(loss_list))


def solution(mesh):
    placed = (
        P(("grp", "wide"), None),
        P(("grp", "wide")),
        P(("grp", "wide"), None),
        P(("grp", "wide")),
        P(),
        P(None, ("grp", "wide")),
        P(None, ("grp", "wide")),
    )
    return jax.shard_map(
        shards,
        mesh=mesh,
        in_specs=placed,
        out_specs=(
            P(("grp", "wide"), None),
            P(("grp", "wide")),
            P(("grp", "wide"), None),
            P(("grp", "wide")),
            P(None, ("grp", "wide")),
        ),
        check_vma=False,
    )
```

profile of v0, /device:TPU:32, one launch (start us, length us, event | category | flops | bytes accessed | tf_op | source)
XLA Modules:
  0.0 493.7 jit_solution(9824283437279981220)
XLA Ops:
  10.7 2.8 copy.34
  13.6 4.9 gather_fusion
  18.5 2.5 multiply_convert_fusion.1
  21.0 72.0 %all-gather.3.cloned.1.call-done = bf16[2048,400]{1,0:T(8,128)(2,1)} async-done(((bf16[64,400]{1,0:T(8,128)(2,1)}), bf16[2048,400]{1,0:T(8,128)(2,1)}) %all-gather.3.cloned.1.call-update) | async-done | bytes 1638416 | tf_op jit(solution)/shard_map/all_gather | solution.py:57
  94.4 31.9 %while.30 = (s32[]{:T(128)}, f32[2048,400]{0,1:T(8,128)}, f32[2,512]{1,0:T(2,128)S(1)}, f32[2,512,400]{1,2,0:T(8,128)}, bf16[2,512,400]{2,1,0:T(8,128)(2,1)S(1)}...) while((s32[]{:T(128)}, f32[2048,400]{0,1:T(8,128)}, ...), condition=%wide.region_4.6_spmd.clone, body=%wide.region_0.5_spmd.clone.sunk | while | flops 2530803200 | bytes 31064192 | solution.py:49
  94.4 3.0 fusion.60
  98.8 2.5 subtract_convert_fusion.4
  101.3 4.4 select_add_fusion.4
  105.7 4.2 fusion.61
  109.9 3.0 fusion.60
  114.3 2.5 subtract_convert_fusion.4
  116.8 5.3 %select_add_fusion.4 = f32[2048,400]{0,1:T(8,128)} fusion(f32[2048,400]{0,1:T(8,128)} %get-tuple-element.322, bf16[512,2048]{1,0:T(8,128)(2,1)} %subtract_convert_fusion.4, pred[]{:T(512)S(6)} %compare.6, bf16[2,512,400]{2,1,0:T(8,128)(2,1)S(1)} %get-tuple-element.334, s32[]{:T(128)S(6)} %copy.55), kind=kOutput, calls=%fused_computation.7.clone.1 | convolution fusion | flops 840499200 | bytes 9175045 | tf_op jit(solution)/shard_map/while/body/eval_jaxpr/sb,sd->bd/dot_general | solution.py:39
  122.2 4.2 fusion.61
  126.4 3.4 convert_element_type.39
  129.8 3.8 copy.41
  133.8 116.0 %reduce-scatter.7.cloned.1.call-done = bf16[64,400]{1,0:T(8,128)(2,1)} async-done(((bf16[2048,400]{1,0:T(8,128)(2,1)}), bf16[64,400]{1,0:T(8,128)(2,1)}) %reduce-scatter.7.cloned.1.call-update) | async-done | bytes 51216
  251.6 7.3 %collective-permute-done = f32[64,400]{0,1:T(8,128)S(1)} collective-permute-done((f32[64,400]{0,1:T(8,128)S(1)}, f32[64,400]{0,1:T(8,128)S(1)}, u32[]{:S(2)}, u32[]{:S(2)}) %collective-permute-start) | collective-permute-done | bytes 102432 | tf_op jit(solution)/shard_map/ppermute | solution.py:15
  259.9 4.9 gather_fusion.1
  264.8 3.0 copy.33
  270.8 3.3 multiply_convert_fusion
  274.1 61.9 %all-gather.5.cloned.1.call-done = bf16[2048,400]{1,0:T(8,128)(2,1)} async-done(((bf16[64,400]{1,0:T(8,128)(2,1)}), bf16[2048,400]{1,0:T(8,128)(2,1)}) %all-gather.5.cloned.1.call-update) | async-done | bytes 1638416 | tf_op jit(solution)/shard_map/all_gather | solution.py:57
  337.4 26.5 %while.31 = (s32[]{:T(128)}, f32[2048,400]{0,1:T(8,128)}, f32[2,512]{1,0:T(2,128)S(1)}, f32[2,512,400]{1,2,0:T(8,128)}, bf16[2,512,400]{2,1,0:T(8,128)(2,1)S(1)}...) while((s32[]{:T(128)}, f32[2048,400]{0,1:T(8,128)}, ...), condition=%wide.region_12.14_spmd.clone, body=%wide.region_8.13_spmd.clone.sunk | while | flops 2530803200 | bytes 31064192 | solution.py:49
  337.4 3.0 fusion.67
  343.4 2.8 select_add_fusion.5
  346.2 3.5 fusion.68
  349.7 3.0 fusion.67
  355.7 4.7 select_add_fusion.5
  360.4 3.5 fusion.68
  366.1 2.4 copy.43
  369.3 2.9 copy.38
  376.8 2.8 copy.39
  380.2 104.7 %reduce-scatter.9.cloned.1.call-done = bf16[64,400]{1,0:T(8,128)(2,1)} async-done(((bf16[2048,400]{1,0:T(8,128)(2,1)}), bf16[64,400]{1,0:T(8,128)(2,1)}) %reduce-scatter.9.cloned.1.call-update) | async-done | bytes 51216
  (87 shorter events, 31.6 us)
Async XLA Ops:
  7.2 85.9 %all-gather.3.cloned.1.call-start = ((), (), s32[]{:S(2)}) async-start(), calls=%async_computation.2 | async-start | bytes 2162688 | tf_op jit(solution)/shard_map/all_gather | solution.py:57
  8.8 241.1 %reduce-scatter.7.cloned.1.call-start = ((), (), s32[]{:S(2)}) async-start(), calls=%async_computation.4 | async-start | bytes 2162688
  10.7 2.9 copy-start.8
  10.7 2.9 copy-start.9
  129.8 3.9 copy-start.6
  133.6 117.3 %copy-start.10 = (f32[64]{0:T(128)S(1)}, f32[64]{0:T(128)}, u32[]{:S(2)}) copy-start(f32[64]{0:T(128)} %param.16) | copy-start | bytes 772
  133.6 202.4 %all-gather.5.cloned.1.call-start = ((), (), s32[]{:S(2)}) async-start(), calls=%async_computation.3 | async-start | bytes 2162688 | tf_op jit(solution)/shard_map/all_gather | solution.py:57
  250.9 7.9 %collective-permute-start = (f32[64,400]{0,1:T(8,128)S(1)}, f32[64,400]{0,1:T(8,128)S(1)}, u32[]{:S(2)}, u32[]{:S(2)}) collective-permute-start(f32[64,400]{0,1:T(8,128)S(1)} %fusion.19), channel_id=1, source_target_pairs={{224,0},{0,32},{32,64},{64,96},{96,128},{128,160},{160,192},{192,2... | collective-permute-start | bytes 307208 | tf_op jit(solution)/shard_map/ppermute | solution.py:15
  259.6 225.2 %reduce-scatter.9.cloned.1.call-start = ((), (), s32[]{:S(2)}) async-start(), calls=%async_computation.5 | async-start | bytes 2162688
  264.8 3.1 copy-start
  267.9 2.3 copy-start.7
  267.9 2.3 copy-start.1
  267.9 2.9 copy-start.3
  368.6 3.6 copy-start.2
  368.6 117.3 %collective-permute-start.1 = (f32[64]{0:T(128)S(1)}, f32[64]{0:T(128)S(1)}, u32[]{:S(2)}, u32[]{:S(2)}) collective-permute-start(f32[64]{0:T(128)S(1)} %get-tuple-element.199), channel_id=1, source_target_pairs={{224,0},{0,32},{32,64},{64,96},{96,128},{128,160},{160,192},{192,2... | collective-permute-start | bytes 776 | tf_op jit(solution)/shard_map/ppermute | solution.py:15
  372.1 2.8 copy-start.4
  372.1 2.9 copy-start.5
Sparse Core Ops, SparseCore 0:
  11.3 81.6 all-gather.2
  133.7 116.0 reduce-scatter.6
  259.8 76.2 all-gather.4
  368.7 116.0 reduce-scatter.8
where the time goes:
time: 496 us; the launch traced here: 494 us
  waiting for transfers between devices  362 us (73%)
  matrix products  44.4 us (9%)
  local copies, waits for them, and re-layouts  36.6 us (7%)
  other arithmetic  35 us (7%)
  between operations  14 us (3%)
    unnamed x6, waiting for transfers between devices  221 us
    all_gather x2, waiting for transfers between devices, shards(): lax.all_gather(dst_rows.astype(jnp.bfloat16), 'wide', axis=0, tiled=True)  134 us
    unnamed x33, local copies, waits for them, and re-layouts  17.2 us
    dot_general x4, matrix products, visit(): jnp.einsum('sb,sd->bd', residual, query, preferred_element_type=jnp.float32)  17.1 us
    dot_general x4, matrix products, visit(): grad_query = jnp.dot(residual, key_rows, preferred_element_type=jnp.float32)  15.4 us
    dot_general x4, matrix products, visit(): jnp.einsum('sd,bd->sb', query, key_rows, preferred_element_type=jnp.float32)  11.8 us
  transfers between devices with their start and end apart: 6, of which 5 were waited for; matrix products, arithmetic and copies ran while one was open for 8% of the time, Pallas kernels for 0%

commit v1 on v0

v1 whole, which is shorter than its diff:
```python
import functools

import jax
import jax.numpy as jnp
from jax import lax
from jax.experimental import pallas as pl
from jax.experimental.pallas import tpu as pltpu
from jax.sharding import PartitionSpec as P

MESH = pl.DeviceIdType.MESH
F32, BF16, I32 = jnp.float32, jnp.bfloat16, jnp.int32
LEARN_RATE = 0.1
D, DP = 400, 512
SRC, BUCKET, SHARD = 1024, 2048, 64
NZ, CHIPS = 8, 16
FLOWS = ((0, 1, 4), (1, -1, 4), (0, -1, 3), (1, 1, 3))
NEED = (4, -4, 3, -3, 2, -2, 1, -1, 0)


def place():
    g, w = lax.axis_index("grp"), lax.axis_index("wide")
    core = lax.rem(w, 2)
    z = lax.rem(lax.div(w, 2), NZ)
    y = lax.div(w, 2 * NZ)
    return g, y, z, core


def wide_of(y, z, core):
    return (y * NZ + z) * 2 + core


def wrap(z):
    return lax.rem(z + 2 * NZ, NZ)


def neighbours(y, z, core):
    return (
        wide_of(1 - y, z, core),
        wide_of(y, z, 1 - core),
        wide_of(y, wrap(z + 1), core),
        wide_of(y, wrap(z - 1), core),
    )


def greet(g, y, z, core, shift=False):
    barrier = pltpu.get_barrier_semaphore()
    targets = [(g, w) for w in neighbours(y, z, core)]
    if shift:
        me = wide_of(y, z, core)
        n = lax.axis_size("grp")
        targets += [(lax.rem(g + 1, n), me), (lax.rem(g + n - 1, n), me)]
    for target in targets:
        pl.semaphore_signal(barrier, inc=1, device_id=target, device_id_type=MESH)
    pl.semaphore_wait(barrier, len(targets))


def remote(src, dst, send, recv, target):
    return pltpu.make_async_remote_copy(
        src_ref=src, dst_ref=dst, send_sem=send, recv_sem=recv,
        device_id=target, device_id_type=MESH,
    )


def gather_keys(keys, ring_s, ring_r, pair_s, pair_r, g, y, z, core):
    yw, cw, rw, lw = neighbours(y, z, core)
    sent = []

    def push(slot, send, recv, w):
        copy = remote(keys.at[slot], keys.at[slot], send, recv, (g, w))
        copy.start()
        sent.append(copy)

    def landed(slot, send, recv, w):
        remote(keys.at[slot], keys.at[slot], send, recv, (g, w)).wait_recv()

    own = wide_of(y, z, core)
    other = wide_of(1 - y, z, core)
    push(own, ring_s.at[16], ring_r.at[16], yw)
    for f, (col, way, hops) in enumerate(FLOWS):
        if col == 0:
            push(own, ring_s.at[4 * f], ring_r.at[4 * f], rw if way > 0 else lw)
    push(own, pair_s.at[0], pair_r.at[0], cw)
    landed(other, ring_s.at[16], ring_r.at[16], yw)
    for f, (col, way, hops) in enumerate(FLOWS):
        if col == 1:
            push(other, ring_s.at[4 * f], ring_r.at[4 * f], rw if way > 0 else lw)
    push(other, pair_s.at[1], pair_r.at[1], cw)
    count = 2
    for k in range(4):
        for f, (col, way, hops) in enumerate(FLOWS):
            if k >= hops:
                continue
            column = y if col == 0 else 1 - y
            slot = wide_of(column, wrap(z - way * (k + 1)), core)
            landed(slot, ring_s.at[4 * f + k], ring_r.at[4 * f + k], lw)
            if k + 1 < hops:
                push(slot, ring_s.at[4 * f + k + 1], ring_r.at[4 * f + k + 1], rw if way > 0 else lw)
            push(slot, pair_s.at[count], pair_r.at[count], cw)
            count += 1
    landed(wide_of(y, z, 1 - core), pair_s.at[0], pair_r.at[0], cw)
    landed(wide_of(1 - y, z, 1 - core), pair_s.at[1], pair_r.at[1], cw)
    count = 2
    for k in range(4):
        for f, (col, way, hops) in enumerate(FLOWS):
            if k >= hops:
                continue
            column = y if col == 0 else 1 - y
            landed(wide_of(column, wrap(z - way * (k + 1)), 1 - core), pair_s.at[count], pair_r.at[count], cw)
            count += 1
    for copy in sent:
        copy.wait_send()


def scatter_sums(part, from_pair, out_sum, ring_in, ring_s, ring_r, pair_s, pair_r, g, y, z, core):
    yw, cw, rw, lw = neighbours(y, z, core)
    sent = []

    def chip(col, dz):
        return (y if col == 0 else 1 - y) * NZ + wrap(z + dz)

    order = []
    for k in range(4):
        for col, way, hops in FLOWS:
            if k < hops:
                order.append((col, way * (hops - k)))
    order += [(1, 0), (0, 0)]
    spot = {key: n for n, key in enumerate(order)}
    for n, (col, dz) in enumerate(order):
        q = chip(col, dz)
        copy = remote(part.at[1 - core, q], from_pair.at[q], pair_s.at[n], pair_r.at[n], (g, cw))
        copy.start()
        sent.append(copy)

    def mine(col, dz):
        q, n = chip(col, dz), spot[(col, dz)]
        remote(part.at[1 - core, q], from_pair.at[q], pair_s.at[n], pair_r.at[n], (g, cw)).wait_recv()
        return part[core, q].astype(F32) + from_pair[q].astype(F32)

    def arrived(f, k):
        remote(ring_in.at[4 * f + k], ring_in.at[4 * f + k], ring_s.at[4 * f + k], ring_r.at[4 * f + k], (g, lw)).wait_recv()
        return ring_in[4 * f + k].astype(F32)

    for k in range(4):
        for f, (col, way, hops) in enumerate(FLOWS):
            if k >= hops:
                continue
            total = mine(col, way * (hops - k))
            if k:
                total = total + arrived(f, k - 1)
            out_sum[4 * f + k] = total.astype(BF16)
            copy = remote(out_sum.at[4 * f + k], ring_in.at[4 * f + k], ring_s.at[4 * f + k], ring_r.at[4 * f + k], (g, rw if way > 0 else lw))
            copy.start()
            sent.append(copy)
    total = mine(1, 0) + arrived(1, 3) + arrived(3, 2)
    out_sum[16] = total.astype(BF16)
    copy = remote(out_sum.at[16], ring_in.at[16], ring_s.at[16], ring_r.at[16], (g, yw))
    copy.start()
    sent.append(copy)
    total = mine(0, 0) + arrived(0, 3) + arrived(2, 2)
    copy.wait_recv()
    total = total + ring_in[16].astype(F32)
    for copy in sent:
        copy.wait_send()
    return total


def column_of(row):
    n = row.shape[1]
    same = lax.broadcasted_iota(I32, (n, n), 0) == lax.broadcasted_iota(I32, (n, n), 1)
    return jnp.sum(jnp.where(same, row, 0.0), axis=1, keepdims=True)


def row_of(column):
    n = column.shape[0]
    same = lax.broadcasted_iota(I32, (n, n), 0) == lax.broadcasted_iota(I32, (n, n), 1)
    return jnp.sum(jnp.where(same, column, 0.0), axis=0, keepdims=True)


def adagrad_rows(rows, accum, grad):
    accum = accum + jnp.sum(grad * grad, axis=1, keepdims=True) * (1.0 / D)
    return rows - (LEARN_RATE * grad) / jnp.sqrt(accum), accum


def first_kernel(rows, keys, ring_s, ring_r, pair_s, pair_r):
    g, y, z, core = place()
    own = wide_of(y, z, core)
    keys[own] = jnp.zeros((SHARD, DP), BF16)
    keys[own, :, 0:D] = rows[...].astype(BF16)
    greet(g, y, z, core)
    gather_keys(keys, ring_s, ring_r, pair_s, pair_r, g, y, z, core)


def middle_kernel(part, rows, accum, keys, new_rows, new_accum,
                  from_pair, out_sum, ring_in, moved, landing,
                  ring_s, ring_r, pair_s, pair_r, ring_s2, ring_r2, pair_s2, pair_r2, move_s, move_r):
    g, y, z, core = place()
    own = wide_of(y, z, core)
    n = lax.axis_size("grp")
    greet(g, y, z, core, shift=True)
    grad = scatter_sums(part, from_pair, out_sum, ring_in, ring_s, ring_r, pair_s, pair_r, g, y, z, core)[:, 0:D]
    updated, total = adagrad_rows(rows[...], column_of(accum[...]), grad)
    moved[:, 384:512] = jnp.broadcast_to(total, (SHARD, 128))
    moved[:, 0:D] = updated
    copy = remote(moved, landing, move_s, move_r, (lax.rem(g + 1, n), own))
    copy.start()
    copy.wait()
    new_rows[...] = landing[:, 0:D]
    new_accum[...] = row_of(landing[:, D:D + 1])
    keys[own] = jnp.zeros((SHARD, DP), BF16)
    keys[own, :, 0:D] = landing[:, 0:D].astype(BF16)
    gather_keys(keys, ring_s2, ring_r2, pair_s2, pair_r2, g, y, z, core)


def last_kernel(part, rows, accum, new_rows, new_accum,
                from_pair, out_sum, ring_in, ring_s, ring_r, pair_s, pair_r):
    g, y, z, core = place()
    greet(g, y, z, core)
    grad = scatter_sums(part, from_pair, out_sum, ring_in, ring_s, ring_r, pair_s, pair_r, g, y, z, core)[:, 0:D]
    updated, total = adagrad_rows(rows[...], column_of(accum[...]), grad)
    new_rows[...] = updated
    new_accum[...] = row_of(total)


CHUNK = 512


def score_kernel(src, accum, rels, ids, labels, keys, new_src, new_accum, loss, part,
                 scale, query_t, query, logits, resid, keys_t):
    for t in range(4):
        lanes = slice(256 * t, 256 * t + 256)
        hot = (lax.broadcasted_iota(I32, (SRC, 256), 0) == ids[:, lanes]).astype(BF16)
        total = jnp.zeros((D, 256), F32)
        rest = rels[...]
        for _ in range(3):
            piece = rest.astype(BF16)
            rest = rest - piece.astype(F32)
            total = total + jnp.dot(piece, hot, preferred_element_type=F32)
        scale[:, lanes] = total
    query_t[D:DP] = jnp.zeros((DP - D, SRC), BF16)
    query_t[0:D] = (src[...] * scale[...]).astype(BF16)
    query[...] = query_t[...].T

    def score(j, top):
        at = pl.ds(pl.multiple_of(j * CHUNK, CHUNK), CHUNK)
        rows = keys[at]
        keys_t[:, at] = rows.T
        block = jnp.dot(rows, query_t[...], preferred_element_type=F32)
        logits[at] = block
        return jnp.maximum(top, jnp.max(block.reshape(CHUNK // 8, 8, SRC), axis=0))

    top = lax.fori_loop(0, BUCKET // CHUNK, score, jnp.full((8, SRC), -jnp.inf, F32))
    top = jnp.max(top, axis=0, keepdims=True)

    def weigh(j, sums):
        at = pl.ds(pl.multiple_of(j * CHUNK, CHUNK), CHUNK)
        block = logits[at]
        hit = lax.broadcasted_iota(I32, (CHUNK, SRC), 0) == labels[...] - j * CHUNK
        powers = jnp.exp(block - top)
        logits[at] = powers
        total, picked = sums
        total = total + jnp.sum(powers.reshape(CHUNK // 8, 8, SRC), axis=0)
        picked = picked + jnp.sum(jnp.where(hit, block, 0.0).reshape(CHUNK // 8, 8, SRC), axis=0)
        return total, picked

    zeros = jnp.zeros((8, SRC), F32)
    total, picked = lax.fori_loop(0, BUCKET // CHUNK, weigh, (zeros, zeros))
    total = jnp.sum(total, axis=0, keepdims=True)
    picked = jnp.sum(picked, axis=0, keepdims=True)
    loss[...] = top + jnp.log(total) - picked
    inverse = 1.0 / total

    def spread(j, _):
        at = pl.ds(pl.multiple_of(j * CHUNK, CHUNK), CHUNK)
        hit = lax.broadcasted_iota(I32, (CHUNK, SRC), 0) == labels[...] - j * CHUNK
        share = logits[at] * inverse
        block = jnp.where(hit, share - 1.0, share).astype(BF16)
        resid[at] = block
        grad = jnp.dot(block, query[...], preferred_element_type=F32).astype(BF16)
        chips = CHUNK // (2 * SHARD)
        for q in range(chips):
            for core in range(2):
                first = (2 * q + core) * SHARD
                part[core, j * chips + q] = grad[first:first + SHARD]
        return 0

    lax.fori_loop(0, BUCKET // CHUNK, spread, 0)
    for t in range(4):
        lanes = slice(256 * t, 256 * t + 256)
        grad = jnp.dot(keys_t[0:D], resid[:, lanes], preferred_element_type=F32) * scale[:, lanes]
        sums = accum[:, lanes] + jnp.sum(grad * grad, axis=0, keepdims=True) * (1.0 / D)
        new_accum[:, lanes] = sums
        new_src[:, lanes] = src[:, lanes] - (LEARN_RATE * grad) / jnp.sqrt(sums)


VM = pl.BlockSpec(memory_space=pltpu.VMEM)
DMA = pltpu.SemaphoreType.DMA
RING = [DMA((17,)), DMA((17,)), DMA((16,)), DMA((16,))]
BUFFERS = [
    pltpu.VMEM((CHIPS, SHARD, DP), BF16),
    pltpu.VMEM((17, SHARD, DP), BF16),
    pltpu.VMEM((17, SHARD, DP), BF16),
]


def call(body, shapes, inputs, scratch, collective=None, cost=None):
    return pl.pallas_call(
        body,
        out_shape=[jax.ShapeDtypeStruct(s, t) for s, t in shapes],
        in_specs=[VM] * inputs,
        out_specs=[VM] * len(shapes),
        scratch_shapes=scratch,
        compiler_params=pltpu.CompilerParams(
            collective_id=collective, has_side_effects=collective is not None,
            vmem_limit_bytes=60 * 1024 * 1024,
        ),
    )


def score(src, accum, rels, ids, labels, keys):
    return call(
        score_kernel,
        [((D, SRC), F32), ((1, SRC), F32), ((1, SRC), F32), ((2, CHIPS, SHARD, DP), BF16)],
        6,
        [
            pltpu.VMEM((D, SRC), F32), pltpu.VMEM((DP, SRC), BF16), pltpu.VMEM((SRC, DP), BF16),
            pltpu.VMEM((BUCKET, SRC), F32), pltpu.VMEM((BUCKET, SRC), BF16), pltpu.VMEM((DP, BUCKET), BF16),
        ],
    )(src, accum, rels, ids, labels, keys.reshape(BUCKET, DP))


def shards(src_rows, src_accum, dst_rows, dst_accum, relations, rel_ids, targets):
    src, rels = src_rows.T, relations.T
    accum = src_accum.reshape(1, SRC)
    (keys,) = call(first_kernel, [((32, SHARD, DP), BF16)], 1, RING, 0)(dst_rows)
    src, accum, loss0, part = score(src, accum, rels, rel_ids[0:1], targets[0:1], keys)
    keys, dst_rows, dst_accum = call(
        middle_kernel,
        [((32, SHARD, DP), BF16), ((SHARD, D), F32), ((1, SHARD), F32)],
        3,
        BUFFERS + [pltpu.VMEM((SHARD, DP), F32)] * 2 + RING + RING + [DMA(()), DMA(())],
        1,
    )(part, dst_rows, dst_accum.reshape(1, SHARD))
    src, accum, loss1, part = score(src, accum, rels, rel_ids[1:2], targets[1:2], keys)
    dst_rows, dst_accum = call(
        last_kernel, [((SHARD, D), F32), ((1, SHARD), F32)], 3, BUFFERS + RING, 2
    )(part, dst_rows, dst_accum)
    return (src.T, accum.reshape(SRC), dst_rows, dst_accum.reshape(SHARD), jnp.concatenate([loss0, loss1], axis=0))


def solution(mesh):
    both = ("grp", "wide")
    placed = (P(both, None), P(both), P(both, None), P(both), P(), P(None, both), P(None, both))
    return jax.shard_map(
        shards, mesh=mesh, in_specs=placed,
        out_specs=(P(both, None), P(both), P(both, None), P(both), P(None, both)),
        check_vma=False,
    )
```

time: 496 us -> 148 us (0.30)
  waiting for transfers between devices: 362 us -> 0 us
  Pallas kernels: 0 us -> 143 us
  matrix products: 44.4 us -> 0 us
  other arithmetic: 35 us -> 0.61 us
  local copies, waits for them, and re-layouts: 36.6 us -> 4.1 us
  between operations: 14 us -> 0.68 us
    unnamed x6 -> x0, waiting for transfers between devices: 221 us -> none
    pallas_call x0 -> x5, Pallas kernels: none -> 143 us  [the longest x1 54.1 us: shards(): call(middle_kernel, [((32, SHARD, DP), BF16), ((SHARD, D), F32), ((1, SHA...]
    all_gather x2 -> x0, waiting for transfers between devices: 134 us -> none  [shards(): lax.all_gather(dst_rows.astype(jnp.bfloat16), 'wide', axis=0, tiled=True)]
    dot_general x12 -> x0, matrix products: 44.4 us -> none  [the longest x4 17.1 us: visit(): jnp.einsum('sb,sd->bd', residual, query, preferred_element_type=jnp.float32)]
    convert_element_type x10 -> x0, other arithmetic: 21.1 us -> none  [the longest x4 8.16 us: visit(): (exp_scores / exp_total - target_hit.astype(jnp.float32)).astype(jnp.bflo...]
    unnamed x33 -> x6, local copies, waits for them, and re-layouts: 17.2 us -> 2.7 us
    reduce_sum x8 -> x0, other arithmetic: 10.3 us -> none  [the longest x4 5.65 us: visit(): picked = jnp.sum(jnp.where(target_hit, logits, 0.0), axis=1)]
    gather x2 -> x0, local copies, waits for them, and re-layouts: 9.8 us -> none  [shards(): rel_scales = jnp.take(relations, rel_ids[round_index], axis=0)]
  transfers between devices with their start and end apart: 6 -> 0, of which waited for: 5 -> 0; matrix products, arithmetic and copies ran while one was open for 8% -> 0% of each run, Pallas kernels for 0% -> 0%
where the time goes in v1:
time: 148 us
  Pallas kernels  143 us (97%)
  local copies, waits for them, and re-layouts  4.1 us (3%)
    pallas_call x1, Pallas kernels, shards(): call(middle_kernel, [((32, SHARD, DP), BF16), ((SHARD, D), F32), ((1, SHA...  54.1 us
    pallas_call x2, Pallas kernels, score(): call(score_kernel, [((D, SRC), F32), ((1, SRC), F32), ((1, SRC), F32), ((...  34.3 us
    pallas_call x1, Pallas kernels, shards(): keys, = call(first_kernel, [((32, SHARD, DP), BF16)], 1, RING, 0)(dst_rows)  28.1 us
    pallas_call x1, Pallas kernels, shards(): call(last_kernel, [((SHARD, D), F32), ((1, SHARD), F32)], 3, BUFFERS + RI...  26 us

profile of v1, /device:TPU:32, one launch (start us, length us, event | category | flops | bytes accessed | tf_op | source)
XLA Modules:
  0.0 147.9 jit_solution(9861900326858069037)
XLA Ops:
  0.6 1.4 fusion
  2.0 28.1 %shard_map.110 = bf16[32,64,512]{2,1,0:T(8,128)(2,1)} custom-call(f32[64,400]{1,0:T(8,128)} %rows.3), custom_call_target="tpu_custom_call" | custom-call | tf_op jit(solution)/shard_map/pallas_call | solution.py:334
  30.2 17.2 %shard_map.111 = (f32[400,1024]{1,0:T(8,128)}, f32[1,1024]{1,0:T(1,128)}, f32[1,1024]{1,0:T(1,128)}, bf16[2,16,64,512]{3,2,1,0:T(8,128)(2,1)}) custom-call(f32[400,1024]{1,0:T(8,128)} %bitcast.13, f32[1,1024]{1,0:T(1,128)} %bitcast.14, f32[400,1024]{1,0:T(8,128)} %bitcast.10, s32[1,1024]{1,0:T(1,128)} %get-tuple-element.35.ids, ...), custom_call_target="tpu_custom_call" | custom-call | tf_op jit(solution)/shard_map/pallas_call | solution.py:320
  47.4 54.1 %shard_map.112 = (bf16[32,64,512]{2,1,0:T(8,128)(2,1)}, f32[64,400]{1,0:T(8,128)}, f32[1,64]{1,0:T(1,128)}) custom-call(bf16[2,16,64,512]{3,2,1,0:T(8,128)(2,1)} %get-tuple-element.20.part, f32[64,400]{1,0:T(8,128)} %rows.3, f32[1,64]{1,0:T(1,128)} %bitcast.15), custom_call_target="tpu_custom_call" | custom-call | tf_op jit(solution)/shard_map/pallas_call | solution.py:336
  101.6 17.0 %shard_map.113 = (f32[400,1024]{1,0:T(8,128)}, f32[1,1024]{1,0:T(1,128)}, f32[1,1024]{1,0:T(1,128)}, bf16[2,16,64,512]{3,2,1,0:T(8,128)(2,1)}) custom-call(f32[400,1024]{1,0:T(8,128)} %get-tuple-element.18.src, f32[1,1024]{1,0:T(1,128)} %get-tuple-element.19.accum, f32[400,1024]{1,0:T(8,128)} %bitcast.11, s32[1,1024]{1,0:T(1,128)} %get-tuple-element.36.ids, ...), custom_call_target="tpu_custom_call" | custom-call | tf_op jit(solution)/shard_map/pallas_call | solution.py:320
  118.6 0.0 copy-start
  118.6 0.0 copy-start.1
  118.6 26.0 %shard_map.114 = (f32[64,400]{1,0:T(8,128)}, f32[1,64]{1,0:T(1,128)}) custom-call(bf16[2,16,64,512]{3,2,1,0:T(8,128)(2,1)} %get-tuple-element.24.part, f32[64,400]{1,0:T(8,128)} %get-tuple-element.25.rows, f32[1,64]{1,0:T(1,128)} %get-tuple-element.26.accum), custom_call_target="tpu_custom_call" | custom-call | tf_op jit(solution)/shard_map/pallas_call | solution.py:344
  144.6 0.0 copy-done
  144.6 0.0 copy-done.1
  144.6 0.6 pad_maximum_fusion
  145.2 1.6 %copy.14 = f32[64,400]{1,0:T(8,128)} copy(f32[64,400]{1,0:T(8,128)} %get-tuple-element.44) | data formatting | bytes 204800
  146.8 1.1 copy.15
Async XLA Ops:
  118.6 26.0 %copy-start = (f32[1,1024]{1,0:T(1,128)S(1)}, f32[1,1024]{1,0:T(1,128)}, u32[]{:S(2)}) copy-start(f32[1,1024]{1,0:T(1,128)} %get-tuple-element.29) | copy-start | bytes 12292
  118.6 26.0 %copy-start.1 = (f32[1,1024]{1,0:T(1,128)S(1)}, f32[1,1024]{1,0:T(1,128)}, u32[]{:S(2)}) copy-start(f32[1,1024]{1,0:T(1,128)} %get-tuple-element.30) | copy-start | bytes 12292

commit v2 on v0

v2 whole, which is shorter than its diff:
```python
import jax
import jax.numpy as jnp
from jax import lax
from jax.experimental import pallas as pl
from jax.experimental.pallas import tpu as pltpu
from jax.sharding import PartitionSpec as P

MESH = pl.DeviceIdType.MESH
F32, BF16, I32 = jnp.float32, jnp.bfloat16, jnp.int32
LEARN_RATE = 0.1
D, DP = 400, 512
SRC, BUCKET, SHARD = 1024, 2048, 64
NZ, CHIPS = 8, 16
BLOCKS = (
    (1, -4), (1, 3), (1, -3), (1, 2),
    (0, 4), (0, -3), (0, 3), (0, -2),
    (1, -2), (1, 1), (1, -1), (1, 0),
    (0, 2), (0, -1), (0, 1), (0, 0),
)
SPOT = {(col, dz % NZ): p for p, (col, dz) in enumerate(BLOCKS)}
GROUP = 512
FLOWS = {0: ((1, 4), (-1, 3)), 1: ((-1, 4), (1, 3))}


def spot(col, dz):
    return SPOT[(col, dz % NZ)]


def ring_at(col, f, k):
    return (2 * col + f) * 4 + k


def place():
    g, w = lax.axis_index("grp"), lax.axis_index("wide")
    core = lax.rem(w, 2)
    z = lax.rem(lax.div(w, 2), NZ)
    y = lax.div(w, 2 * NZ)
    return g, y, z, core


def wide_of(y, z, core):
    return (y * NZ + z) * 2 + core


def wrap(z):
    return lax.rem(z + 2 * NZ, NZ)


def neighbours(y, z, core):
    return (
        wide_of(1 - y, z, core),
        wide_of(y, z, 1 - core),
        wide_of(y, wrap(z + 1), core),
        wide_of(y, wrap(z - 1), core),
    )


def greet(g, y, z, core, shift=False):
    barrier = pltpu.get_barrier_semaphore()
    targets = [(g, w) for w in neighbours(y, z, core)]
    if shift:
        me = wide_of(y, z, core)
        n = lax.axis_size("grp")
        targets += [(lax.rem(g + 1, n), me), (lax.rem(g + n - 1, n), me)]
    for target in targets:
        pl.semaphore_signal(barrier, inc=1, device_id=target, device_id_type=MESH)
    pl.semaphore_wait(barrier, len(targets))


def remote(src, dst, send, recv, target):
    return pltpu.make_async_remote_copy(
        src_ref=src, dst_ref=dst, send_sem=send, recv_sem=recv,
        device_id=target, device_id_type=MESH,
    )


class Gather:
    def __init__(self, keys, ring_s, ring_r, pair_s, pair_r, me):
        self.keys, self.sems, self.me, self.sent = keys, (ring_s, ring_r, pair_s, pair_r), me, []

    def copy(self, p, q, n, pair, w):
        g, y, z, core = self.me
        send, recv = self.sems[2:] if pair else self.sems[:2]
        return remote(self.keys.at[2 * p + core], self.keys.at[2 * q + core], send.at[n], recv.at[n], (g, w))

    def push(self, p, q, n, pair, w):
        copy = self.copy(p, q, n, pair, w)
        copy.start()
        self.sent.append(copy)

    def along(self, col, k, p_of):
        g, y, z, core = self.me
        yw, cw, rw, lw = neighbours(y, z, core)
        for f, (way, hops) in enumerate(FLOWS[col]):
            if k < hops:
                self.push(p_of(f, way, k), spot(col, -way * (k + 1)), ring_at(col, f, k), False, rw if way > 0 else lw)

    def start(self):
        g, y, z, core = self.me
        yw, cw, rw, lw = neighbours(y, z, core)
        own = spot(0, 0)
        self.push(own, spot(1, 0), 16, False, yw)
        self.along(0, 0, lambda f, way, k: own)
        self.push(own, own, own, True, cw)

    def across(self):
        g, y, z, core = self.me
        yw, cw, rw, lw = neighbours(y, z, core)
        other = spot(1, 0)
        self.copy(spot(0, 0), other, 16, False, yw).wait_recv()
        self.along(1, 0, lambda f, way, k: other)
        self.push(other, other, other, True, cw)

    def hop(self, col, k):
        g, y, z, core = self.me
        yw, cw, rw, lw = neighbours(y, z, core)
        for f, (way, hops) in enumerate(FLOWS[col]):
            if k >= hops:
                continue
            p = spot(col, -way * (k + 1))
            self.copy(p, p, ring_at(col, f, k), False, lw).wait_recv()
            if k + 1 < hops:
                self.push(p, spot(col, -way * (k + 2)), ring_at(col, f, k + 1), False, rw if way > 0 else lw)
            self.push(p, p, p, True, cw)

    def pair(self, group):
        g, y, z, core = self.me
        yw, cw, rw, lw = neighbours(y, z, core)
        for p in range(4 * group, 4 * group + 4):
            send, recv = self.sems[2:]
            slot = self.keys.at[2 * p + 1 - core]
            remote(slot, slot, send.at[p], recv.at[p], (g, cw)).wait_recv()

    def finish(self):
        for copy in self.sent:
            copy.wait_send()


class Scatter:
    def __init__(self, part, from_pair, out_sum, ring_in, ring_s, ring_r, pair_s, pair_r, me):
        self.part, self.from_pair, self.out_sum, self.ring_in = part, from_pair, out_sum, ring_in
        self.sems, self.me, self.sent = (ring_s, ring_r, pair_s, pair_r), me, []

    def swap(self, p):
        g, y, z, core = self.me
        yw, cw, rw, lw = neighbours(y, z, core)
        return remote(self.part.at[p, 1 - core], self.from_pair.at[p], self.sems[2].at[p], self.sems[3].at[p], (g, cw))

    def pair(self, group):
        for p in range(4 * group, 4 * group + 4):
            copy = self.swap(p)
            copy.start()
            self.sent.append(copy)

    def mine(self, col, dz):
        p = spot(col, dz)
        self.swap(p).wait_recv()
        return self.part[p, self.me[3]].astype(F32) + self.from_pair[p].astype(F32)

    def step(self, n, w):
        return remote(self.out_sum.at[n], self.ring_in.at[n], self.sems[0].at[n], self.sems[1].at[n], (self.me[0], w))

    def arrived(self, n):
        g, y, z, core = self.me
        self.step(n, neighbours(y, z, core)[3]).wait_recv()
        return self.ring_in[n].astype(F32)

    def send(self, n, total, w):
        self.out_sum[n] = total.astype(BF16)
        copy = self.step(n, w)
        copy.start()
        self.sent.append(copy)

    def hop(self, col, k):
        g, y, z, core = self.me
        yw, cw, rw, lw = neighbours(y, z, core)
        for f, (way, hops) in enumerate(FLOWS[col]):
            if k >= hops:
                continue
            total = self.mine(col, way * (hops - k))
            if k:
                total = total + self.arrived(ring_at(col, f, k - 1))
            self.send(ring_at(col, f, k), total, rw if way > 0 else lw)

    def last(self, col):
        total = self.mine(col, 0)
        for f, (way, hops) in enumerate(FLOWS[col]):
            total = total + self.arrived(ring_at(col, f, hops - 1))
        return total

    def across(self):
        g, y, z, core = self.me
        self.send(16, self.last(1), neighbours(y, z, core)[0])

    def finish(self):
        total = self.last(0)
        total = total + self.arrived(16)
        for copy in self.sent:
            copy.wait_send()
        return total


def column_of(row):
    n = row.shape[1]
    same = lax.broadcasted_iota(I32, (n, n), 0) == lax.broadcasted_iota(I32, (n, n), 1)
    return jnp.sum(jnp.where(same, row, 0.0), axis=1, keepdims=True)


def row_of(column):
    n = column.shape[0]
    same = lax.broadcasted_iota(I32, (n, n), 0) == lax.broadcasted_iota(I32, (n, n), 1)
    return jnp.sum(jnp.where(same, column, 0.0), axis=0, keepdims=True)


def adagrad_rows(rows, accum, grad):
    accum = accum + jnp.sum(grad * grad, axis=1, keepdims=True) * (1.0 / D)
    return rows - (LEARN_RATE * grad) / jnp.sqrt(accum), accum


def train_kernel(src, accum, rows, row_accum, rels, ids, labels,
                 new_src, new_accum, new_rows, new_row_accum, loss,
                 scale, query_t, query, logits, resid, keys_t,
                 keys0, keys1, part0, part1, pair0, pair1, out0, out1, in0, in1, key_row, moved, landing, tops,
                 *sems):
    me = g, y, z, core = place()
    here = wide_of(y, z, core)
    beyond = (lax.rem(g + 1, lax.axis_size("grp")), here)
    own = 2 * spot(0, 0) + core

    def tile(t):
        return slice(256 * t, 256 * t + 256)

    def relate(r, t):
        hot = (lax.broadcasted_iota(I32, (SRC, 256), 0) == ids[r:r + 1, tile(t)]).astype(BF16)
        total = jnp.zeros((D, 256), F32)
        rest = rels[...]
        for _ in range(3):
            piece = rest.astype(BF16)
            rest = rest - piece.astype(F32)
            total = total + jnp.dot(piece, hot, preferred_element_type=F32)
        scale[r, :, tile(t)] = total

    def ask(r, t):
        table = src if r == 0 else new_src
        quarter = (table[:, tile(t)] * scale[r, :, tile(t)]).astype(BF16)
        query_t[0:D, tile(t)] = quarter
        query[tile(t), 0:D] = quarter.T

    def hits(r, p):
        col, dz = BLOCKS[p]
        chip = (y if col == 0 else 1 - y) * NZ + wrap(z + dz)
        return lax.broadcasted_iota(I32, (128, SRC), 0) == labels[r:r + 1, :] - 128 * chip

    def fold(x):
        return x.reshape(-1, 8, SRC)

    class Softmax:
        def __init__(self, r, keys):
            self.r, self.keys, self.top = r, keys, None
            self.total = self.picked = None

        def score(self, group):
            rows_ = self.keys[8 * group:8 * group + 8].reshape(GROUP, DP)
            keys_t[:, GROUP * group:GROUP * group + GROUP] = rows_.T
            at = slice(GROUP * group, GROUP * group + GROUP)
            logits[at] = jnp.dot(rows_, query_t[...], preferred_element_type=F32)
            top = jnp.max(jnp.max(fold(logits[at]), axis=0), axis=0, keepdims=True)
            if self.top is not None:
                top = jnp.maximum(top, self.top)
            total = picked = jnp.zeros((8, SRC), F32)
            for p in range(4 * group, 4 * group + 4):
                lines = slice(128 * p, 128 * p + 128)
                block = logits[lines]
                powers = jnp.exp(block - top)
                picked = picked + jnp.sum(fold(jnp.where(hits(self.r, p), block, 0.0)), axis=0)
                total = total + jnp.sum(fold(powers), axis=0)
                logits[lines] = powers
            if self.top is not None:
                total = total + self.total * jnp.exp(self.top - top)
                picked = picked + self.picked
            self.top, self.total, self.picked = top, total, picked
            tops[group:group + 1] = top

        def close(self):
            total = jnp.sum(self.total, axis=0, keepdims=True)
            loss[self.r:self.r + 1] = self.top + jnp.log(total) - jnp.sum(self.picked, axis=0, keepdims=True)
            self.inverse = 1.0 / total

        def spread(self, group, part):
            factor = jnp.exp(tops[group:group + 1] - self.top) * self.inverse
            for p in range(4 * group, 4 * group + 4):
                lines = slice(128 * p, 128 * p + 128)
                share = logits[lines] * factor
                resid[lines] = jnp.where(hits(self.r, p), share - 1.0, share).astype(BF16)
            at = slice(GROUP * group, GROUP * group + GROUP)
            grad = jnp.dot(resid[at], query[...], preferred_element_type=F32).astype(BF16)
            part[4 * group:4 * group + 4] = grad.reshape(4, 2, SHARD, DP)

    def learn(r, t):
        table, totals = (src, accum) if r == 0 else (new_src, new_accum)
        grad = jnp.dot(keys_t[0:D], resid[:, tile(t)], preferred_element_type=F32) * scale[r, :, tile(t)]
        sums = totals[:, tile(t)] + jnp.sum(grad * grad, axis=0, keepdims=True) * (1.0 / D)
        new_accum[:, tile(t)] = sums
        new_src[:, tile(t)] = table[:, tile(t)] - (LEARN_RATE * grad) / jnp.sqrt(sums)

    keys0[own] = jnp.zeros((SHARD, DP), BF16)
    keys0[own, :, 0:D] = rows[...].astype(BF16)
    key_row[...] = jnp.zeros((SHARD, DP), BF16)
    query_t[D:DP] = jnp.zeros((DP - D, SRC), BF16)
    query[:, 384:DP] = jnp.zeros((SRC, DP - 384), BF16)
    greet(g, y, z, core, shift=True)
    gather = Gather(keys0, *sems[0:4], me)
    gather.start()
    relate(0, 0)
    gather.hop(0, 0)
    relate(0, 1)
    gather.across()
    relate(0, 2)
    gather.hop(0, 1)
    relate(0, 3)
    gather.hop(1, 0)
    ask(0, 0)
    ask(0, 1)
    gather.hop(0, 2)
    ask(0, 2)
    ask(0, 3)
    soft = Softmax(0, keys0)

    def rest_of_gather(gather, soft):
        gather.hop(1, 1)
        gather.pair(3)
        soft.score(3)
        gather.hop(0, 3)
        gather.hop(1, 2)
        gather.pair(2)
        soft.score(2)
        gather.hop(1, 3)
        gather.pair(1)
        soft.score(1)
        gather.pair(0)
        soft.score(0)
        soft.close()
        gather.finish()

    rest_of_gather(gather, soft)

    def rest_of_scatter(scatter, soft, part, r):
        soft.spread(0, part)
        scatter.pair(0)
        soft.spread(1, part)
        scatter.pair(1)
        scatter.hop(1, 0)
        soft.spread(2, part)
        scatter.pair(2)
        scatter.hop(0, 0)
        scatter.hop(1, 1)
        soft.spread(3, part)
        scatter.pair(3)
        scatter.hop(0, 1)
        scatter.hop(1, 2)
        learn(r, 0)
        scatter.hop(0, 2)
        scatter.hop(1, 3)
        learn(r, 1)
        scatter.across()
        scatter.hop(0, 3)
        learn(r, 2)
        learn(r, 3)

    scatter = Scatter(part0, pair0, out0, in0, *sems[4:8], me)
    rest_of_scatter(scatter, soft, part0, 0)
    grad = scatter.finish()[:, 0:D]
    updated, total = adagrad_rows(rows[...], column_of(row_accum[...]), grad)
    key_row[:, 0:D] = updated.astype(BF16)
    moved[:, 384:512] = jnp.broadcast_to(total, (SHARD, 128))
    moved[:, 0:D] = updated
    shift = remote(key_row, keys1.at[own], sems[16].at[0], sems[17].at[0], beyond)
    shift.start()
    carry = remote(moved, landing, sems[16].at[1], sems[17].at[1], beyond)
    carry.start()
    relate(1, 0)
    shift.wait_recv()
    gather = Gather(keys1, *sems[8:12], me)
    gather.start()
    relate(1, 1)
    gather.hop(0, 0)
    relate(1, 2)
    gather.across()
    relate(1, 3)
    gather.hop(0, 1)
    ask(1, 0)
    ask(1, 1)
    gather.hop(1, 0)
    gather.hop(0, 2)
    ask(1, 2)
    ask(1, 3)
    soft = Softmax(1, keys1)
    rest_of_gather(gather, soft)
    scatter = Scatter(part1, pair1, out1, in1, *sems[12:16], me)
    rest_of_scatter(scatter, soft, part1, 1)
    grad = scatter.finish()[:, 0:D]
    carry.wait_recv()
    updated, total = adagrad_rows(landing[:, 0:D], landing[:, D:D + 1], grad)
    new_rows[...] = updated
    new_row_accum[...] = row_of(total)
    shift.wait_send()
    carry.wait_send()


VM = pl.BlockSpec(memory_space=pltpu.VMEM)
DMA = pltpu.SemaphoreType.DMA


def shards(src_rows, src_accum, dst_rows, dst_accum, relations, rel_ids, targets):
    twice = lambda shape, kind: [pltpu.VMEM(shape, kind)] * 2
    new_src, new_accum, new_rows, new_row_accum, loss = pl.pallas_call(
        train_kernel,
        out_shape=[
            jax.ShapeDtypeStruct(s, F32) for s in ((D, SRC), (1, SRC), (SHARD, D), (1, SHARD), (2, SRC))
        ],
        in_specs=[VM] * 7,
        out_specs=[VM] * 5,
        scratch_shapes=[
            pltpu.VMEM((2, D, SRC), F32), pltpu.VMEM((DP, SRC), BF16), pltpu.VMEM((SRC, DP), BF16),
            pltpu.VMEM((BUCKET, SRC), F32), pltpu.VMEM((BUCKET, SRC), BF16), pltpu.VMEM((DP, BUCKET), BF16),
            *twice((32, SHARD, DP), BF16), *twice((CHIPS, 2, SHARD, DP), BF16), *twice((CHIPS, SHARD, DP), BF16),
            *twice((17, SHARD, DP), BF16), *twice((17, SHARD, DP), BF16),
            pltpu.VMEM((SHARD, DP), BF16), *twice((SHARD, DP), F32), pltpu.VMEM((8, SRC), F32),
            *([DMA((17,)), DMA((17,)), DMA((16,)), DMA((16,))] * 4), DMA((2,)), DMA((2,)),
        ],
        compiler_params=pltpu.CompilerParams(
            collective_id=0, has_side_effects=True, vmem_limit_bytes=62 * 1024 * 1024,
        ),
    )(src_rows.T, src_accum.reshape(1, SRC), dst_rows, dst_accum.reshape(1, SHARD), relations.T, rel_ids, targets)
    return (new_src.T, new_accum.reshape(SRC), new_rows, new_row_accum.reshape(SHARD), loss)


def solution(mesh):
    both = ("grp", "wide")
    placed = (P(both, None), P(both), P(both, None), P(both), P(), P(None, both), P(None, both))
    return jax.shard_map(
        shards, mesh=mesh, in_specs=placed,
        out_specs=(P(both, None), P(both), P(both, None), P(both), P(None, both)),
        check_vma=False,
    )
```

time: 496 us -> 115 us (0.23)
  waiting for transfers between devices: 362 us -> 0 us
  Pallas kernels: 0 us -> 108 us
  matrix products: 44.4 us -> 0 us
  other arithmetic: 35 us -> 0 us
  local copies, waits for them, and re-layouts: 36.6 us -> 5.21 us
  between operations: 14 us -> 0.68 us
    unnamed x6 -> x0, waiting for transfers between devices: 221 us -> none
    all_gather x2 -> x0, waiting for transfers between devices: 134 us -> none  [shards(): lax.all_gather(dst_rows.astype(jnp.bfloat16), 'wide', axis=0, tiled=True)]
    pallas_call x0 -> x1, Pallas kernels: none -> 108 us  [shards(): pl.pallas_call(train_kernel, out_shape=[jax.ShapeDtypeStruct(s, F32) for...]
    dot_general x12 -> x0, matrix products: 44.4 us -> none  [the longest x4 17.1 us: visit(): jnp.einsum('sb,sd->bd', residual, query, preferred_element_type=jnp.float32)]
    convert_element_type x10 -> x0, other arithmetic: 21.1 us -> none  [the longest x4 8.16 us: visit(): (exp_scores / exp_total - target_hit.astype(jnp.float32)).astype(jnp.bflo...]
    unnamed x33 -> x13, local copies, waits for them, and re-layouts: 17.2 us -> 5.21 us
    reduce_sum x8 -> x0, other arithmetic: 10.3 us -> none  [the longest x4 5.65 us: visit(): picked = jnp.sum(jnp.where(target_hit, logits, 0.0), axis=1)]
    gather x2 -> x0, local copies, waits for them, and re-layouts: 9.8 us -> none  [shards(): rel_scales = jnp.take(relations, rel_ids[round_index], axis=0)]
  transfers between devices with their start and end apart: 6 -> 0, of which waited for: 5 -> 0; matrix products, arithmetic and copies ran while one was open for 8% -> 0% of each run, Pallas kernels for 0% -> 0%
where the time goes in v2:
time: 115 us; the launch traced here: 114 us
  Pallas kernels  108 us (94%)
  local copies, waits for them, and re-layouts  5.21 us (5%)
    pallas_call x1, Pallas kernels, shards(): pl.pallas_call(train_kernel, out_shape=[jax.ShapeDtypeStruct(s, F32) for...  108 us
    unnamed x13, local copies, waits for them, and re-layouts  5.21 us

profile of v2, /device:TPU:32, one launch (start us, length us, event | category | flops | bytes accessed | tf_op | source)
XLA Modules:
  0.0 113.9 jit_solution(1319034107860657614)
XLA Ops:
  0.6 108.0 %shard_map.110 = (f32[400,1024]{1,0:T(8,128)}, f32[1,1024]{1,0:T(1,128)}, f32[64,400]{1,0:T(8,128)}, f32[1,64]{1,0:T(1,128)}, f32[2,1024]{1,0:T(2,128)}) custom-call(f32[400,1024]{1,0:T(8,128)} %bitcast.7, f32[1,1024]{1,0:T(1,128)} %bitcast.10, f32[64,400]{1,0:T(8,128)} %rows.1, f32[1,64]{1,0:T(1,128)} %bitcast.12, f32[400,1024]{1,0:T(8,128)} %bitcast.8, ...), custom_call_target="tpu_custom_call" | custom-call | tf_op jit(solution)/shard_map/pallas_call | solution.py:416
  108.6 0.0 copy-start.2
  108.6 0.0 copy-start
  108.7 0.0 copy-start.3
  108.7 0.0 copy-start.1
  108.7 2.8 %copy.17 = f32[1024,400]{0,1:T(8,128)} copy(f32[1024,400]{0,1:T(8,128)} %bitcast.9) | data formatting | bytes 3276800
  111.5 0.0 copy-done.2
  111.5 0.6 copy.18
  112.1 0.0 copy-done
  112.1 0.7 copy.19
  112.8 0.0 copy-done.3
  112.8 0.5 copy.20
  113.3 0.0 copy-done.1
  113.3 0.6 copy.21
Async XLA Ops:
  108.6 2.9 %copy-start.2 = (f32[1,1024]{1,0:T(1,128)S(1)}, f32[1,1024]{1,0:T(1,128)}, u32[]{:S(2)}) copy-start(f32[1,1024]{1,0:T(1,128)} %get-tuple-element.11) | copy-start | bytes 12292
  108.6 3.5 %copy-start = (f32[64,400]{1,0:T(8,128)S(1)}, f32[64,400]{1,0:T(8,128)}, u32[]{:S(2)}) copy-start(f32[64,400]{1,0:T(8,128)} %get-tuple-element.22) | copy-start | bytes 307204
  108.7 4.1 %copy-start.3 = (f32[1,64]{1,0:T(1,128)S(1)}, f32[1,64]{1,0:T(1,128)}, u32[]{:S(2)}) copy-start(f32[1,64]{1,0:T(1,128)} %get-tuple-element.13) | copy-start | bytes 772
  108.7 4.6 %copy-start.1 = (f32[2,1024]{1,0:T(2,128)S(1)}, f32[2,1024]{1,0:T(2,128)}, u32[]{:S(2)}) copy-start(f32[2,1024]{1,0:T(2,128)} %get-tuple-element.24) | copy-start | bytes 24580

commit v3 on v2

v3 whole, which is shorter than its diff:
```python
import jax
import jax.numpy as jnp
from jax import lax
from jax.experimental import pallas as pl
from jax.experimental.pallas import tpu as pltpu
from jax.sharding import PartitionSpec as P

MESH = pl.DeviceIdType.MESH
F32, BF16, I32 = jnp.float32, jnp.bfloat16, jnp.int32
LEARN_RATE = 0.1
D, DP = 400, 512
SRC, BUCKET, SHARD = 1024, 2048, 64
NZ, CHIPS = 8, 16
GROUPS = (
    ((1, 4), (0, 4)),
    ((1, 3), (1, -3), (0, 3), (0, -3)),
    ((1, 2), (1, -2), (0, 2), (0, -2)),
    ((0, 1), (0, -1), (1, 0), (0, 0), (1, 1), (1, -1)),
)
BLOCKS = sum(GROUPS, ())
SPOT = {(col, dz % NZ): p for p, (col, dz) in enumerate(BLOCKS)}
SPANS = tuple(range(sum(map(len, GROUPS[:n])), sum(map(len, GROUPS[:n + 1]))) for n in range(len(GROUPS)))
SLOT = 208
DIRECT = ((0, 2), (0, -2), (1, 2), (1, -2), (0, 1), (0, -1), (1, 0), (1, 1), (1, -1))
RELAYS = tuple((col, way, more) for col in (0, 1) for way in (1, -1) for more in (1, 2) if more == 1 or way == (1, -1)[col])
STEPS = len(DIRECT) + len(RELAYS) + 1
HOME = STEPS - 1


def spot(col, dz):
    return SPOT[(col, dz % NZ)]


def direct_at(col, dz):
    return DIRECT.index((col, dz))


def relay_at(col, way, more):
    return len(DIRECT) + RELAYS.index((col, way, more))


def pack(x):
    last = x[:, 384:512]
    tail = last[0:16]
    for q in range(1, 4):
        tail = tail + pltpu.roll(last[16 * q:16 * q + 16], 16 * q, 1)
    return jnp.concatenate([x[:, 0:128], x[:, 128:256], x[:, 256:384], tail], axis=0)


def unpack_tail(tail):
    keep = lax.broadcasted_iota(I32, (16, 128), 1) < 16
    parts = [tail] + [pltpu.roll(tail, 128 - 16 * q, 1) for q in range(1, 4)]
    return jnp.concatenate([jnp.where(keep, part, 0.0) for part in parts], axis=0)


def unpack(x):
    return jnp.concatenate([x[0:64], x[64:128], x[128:192], unpack_tail(x[192:208])], axis=1)


def place():
    g, w = lax.axis_index("grp"), lax.axis_index("wide")
    core = lax.rem(w, 2)
    z = lax.rem(lax.div(w, 2), NZ)
    y = lax.div(w, 2 * NZ)
    return g, y, z, core


def wide_of(y, z, core):
    return (y * NZ + z) * 2 + core


def wrap(z):
    return lax.rem(z + 2 * NZ, NZ)


def at(me, col, dz):
    g, y, z, core = me
    return wide_of(y if col == 0 else 1 - y, wrap(z + dz), core)


def greet(me):
    g, y, z, core = me
    n = lax.axis_size("grp")
    barrier = pltpu.get_barrier_semaphore()
    around = [at(me, col, dz) for col, dz in DIRECT]
    targets = [(g, w) for w in around + [wide_of(y, z, 1 - core)]]
    for other in (lax.rem(g + 1, n), lax.rem(g + n - 1, n)):
        targets.append((other, wide_of(y, z, core)))
    for target in targets:
        pl.semaphore_signal(barrier, inc=1, device_id=target, device_id_type=MESH)
    pl.semaphore_wait(barrier, len(targets))


def remote(src, dst, send, recv, target):
    return pltpu.make_async_remote_copy(
        src_ref=src, dst_ref=dst, send_sem=send, recv_sem=recv,
        device_id=target, device_id_type=MESH,
    )


class Gather:
    def __init__(self, keys, step_s, step_r, pair_s, pair_r, me):
        self.keys, self.sems, self.me, self.sent = keys, (step_s, step_r, pair_s, pair_r), me, []

    def copy(self, p, q, n, device, pair=False):
        core = self.me[3]
        send, recv = self.sems[2:] if pair else self.sems[:2]
        return remote(self.keys.at[2 * p + core], self.keys.at[2 * q + core], send.at[n], recv.at[n], device)

    def push(self, *args, **kwargs):
        copy = self.copy(*args, **kwargs)
        copy.start()
        self.sent.append(copy)

    def share(self, p):
        g, y, z, core = self.me
        self.push(p, p, p, (g, wide_of(y, z, 1 - core)), pair=True)

    def start(self):
        own = spot(0, 0)
        for col, dz in DIRECT:
            self.push(own, spot(col, -dz), direct_at(col, dz), (self.me[0], at(self.me, col, dz)))
        self.share(own)

    def wait(self, p, n):
        g, y, z, core = self.me
        self.copy(p, p, n, (g, wide_of(y, z, 1 - core))).wait_recv()

    def relay(self, col):
        for way in (1, -1):
            p = spot(col, -2 * way)
            self.wait(p, direct_at(col, 2 * way))
            for more in (2, 1):
                if (col, way, more) in RELAYS:
                    self.push(p, spot(col, -way * (2 + more)), relay_at(col, way, more), (self.me[0], at(self.me, 0, way * more)))
            self.share(p)

    def near(self, col, dz):
        p = spot(col, -dz)
        self.wait(p, direct_at(col, dz))
        self.share(p)

    def far(self, col, more):
        for way in (1, -1):
            if (col, way, more) in RELAYS:
                p = spot(col, -way * (2 + more))
                self.wait(p, relay_at(col, way, more))
                self.share(p)

    def pair(self, group):
        g, y, z, core = self.me
        for p in SPANS[group]:
            slot = self.keys.at[2 * p + 1 - core]
            remote(slot, slot, self.sems[2].at[p], self.sems[3].at[p], (g, wide_of(y, z, 1 - core))).wait_recv()

    def finish(self):
        for copy in self.sent:
            copy.wait_send()


class Scatter:
    def __init__(self, part, from_pair, out_sum, inbox, step_s, step_r, pair_s, pair_r, me):
        self.part, self.from_pair, self.out_sum, self.inbox = part, from_pair, out_sum, inbox
        self.sems, self.me, self.sent = (step_s, step_r, pair_s, pair_r), me, []

    def swap(self, p):
        g, y, z, core = self.me
        return remote(self.part.at[p, 1 - core], self.from_pair.at[p], self.sems[2].at[p], self.sems[3].at[p],
                      (g, wide_of(y, z, 1 - core)))

    def pair(self, group):
        for p in SPANS[group]:
            copy = self.swap(p)
            copy.start()
            self.sent.append(copy)

    def mine(self, col, dz):
        p = spot(col, dz)
        self.swap(p).wait_recv()
        return self.part[p, self.me[3]].astype(F32) + self.from_pair[p].astype(F32)

    def step(self, n, w):
        return remote(self.out_sum.at[n], self.inbox.at[n], self.sems[0].at[n], self.sems[1].at[n], (self.me[0], w))

    def arrived(self, n):
        self.step(n, at(self.me, 0, 1)).wait_recv()
        return self.inbox[n].astype(F32)

    def send(self, n, total, w):
        self.out_sum[n] = total.astype(BF16)
        copy = self.step(n, w)
        copy.start()
        self.sent.append(copy)

    def far(self, col, more):
        for way in (1, -1):
            if (col, way, more) in RELAYS:
                self.send(relay_at(col, way, more), self.mine(col, way * (2 + more)), at(self.me, 0, way * more))

    def relay(self, col):
        for way in (1, -1):
            total = self.mine(col, 2 * way)
            for more in (1, 2):
                if (col, way, more) in RELAYS:
                    total = total + self.arrived(relay_at(col, way, more))
            self.send(direct_at(col, 2 * way), total, at(self.me, col, 2 * way))

    def near(self, col, dz):
        self.send(direct_at(col, dz), self.mine(col, dz), at(self.me, col, dz))

    def finish(self):
        total = self.mine(0, 0)
        for col, dz in ((0, 1), (0, -1), (1, 0), (1, 1), (1, -1), (0, 2), (0, -2), (1, 2), (1, -2)):
            total = total + self.arrived(direct_at(col, dz))
        for copy in self.sent:
            copy.wait_send()
        return unpack(total)


def column_of(row):
    n = row.shape[1]
    same = lax.broadcasted_iota(I32, (n, n), 0) == lax.broadcasted_iota(I32, (n, n), 1)
    return jnp.sum(jnp.where(same, row, 0.0), axis=1, keepdims=True)


def row_of(column):
    n = column.shape[0]
    same = lax.broadcasted_iota(I32, (n, n), 0) == lax.broadcasted_iota(I32, (n, n), 1)
    return jnp.sum(jnp.where(same, column, 0.0), axis=0, keepdims=True)


def adagrad_rows(rows, accum, grad):
    accum = accum + jnp.sum(grad * grad, axis=1, keepdims=True) * (1.0 / D)
    return rows - (LEARN_RATE * grad) / jnp.sqrt(accum), accum


def train_kernel(src, accum, rows, row_accum, rels, ids, labels,
                 new_src, new_accum, new_rows, new_row_accum, loss,
                 scale, query_t, query, logits, resid, keys_t,
                 keys0, keys1, part0, part1, pair0, pair1, out0, out1, in0, in1, key_row, moved, landing, tops,
                 *sems):
    me = g, y, z, core = place()
    here = wide_of(y, z, core)
    beyond = (lax.rem(g + 1, lax.axis_size("grp")), here)
    own = 2 * spot(0, 0) + core

    def tile(t):
        return slice(256 * t, 256 * t + 256)

    def relate(r, t):
        hot = (lax.broadcasted_iota(I32, (SRC, 256), 0) == ids[r:r + 1, tile(t)]).astype(BF16)
        total = jnp.zeros((D, 256), F32)
        rest = rels[...]
        for _ in range(3):
            piece = rest.astype(BF16)
            rest = rest - piece.astype(F32)
            total = total + jnp.dot(piece, hot, preferred_element_type=F32)
        scale[r, :, tile(t)] = total

    def ask(r, t):
        table = src if r == 0 else new_src
        quarter = (table[:, tile(t)] * scale[r, :, tile(t)]).astype(BF16)
        query_t[0:D, tile(t)] = quarter
        query[tile(t), 0:D] = quarter.T

    def hits(r, p):
        col, dz = BLOCKS[p]
        chip = (y if col == 0 else 1 - y) * NZ + wrap(z + dz)
        return lax.broadcasted_iota(I32, (128, SRC), 0) == labels[r:r + 1, :] - 128 * chip

    def fold(x):
        return x.reshape(-1, 8, SRC)

    class Softmax:
        def __init__(self, r, keys):
            self.r, self.keys, self.top = r, keys, None
            self.total = self.picked = None

        def score(self, group):
            pieces = []
            for s in range(2 * SPANS[group][0], 2 * SPANS[group][-1] + 2):
                end = unpack_tail(self.keys[s, 192:208].astype(F32)).astype(BF16)
                pieces.append(jnp.concatenate([self.keys[s, 0:64], self.keys[s, 64:128], self.keys[s, 128:192], end], axis=1))
            rows_ = jnp.concatenate(pieces, axis=0)
            at = slice(128 * SPANS[group][0], 128 * SPANS[group][-1] + 128)
            keys_t[:, at] = rows_.T
            logits[at] = jnp.dot(rows_, query_t[...], preferred_element_type=F32)
            top = jnp.max(jnp.max(fold(logits[at]), axis=0), axis=0, keepdims=True)
            if self.top is not None:
                top = jnp.maximum(top, self.top)
            total = picked = jnp.zeros((8, SRC), F32)
            for p in SPANS[group]:
                lines = slice(128 * p, 128 * p + 128)
                block = logits[lines]
                powers = jnp.exp(block - top)
                picked = picked + jnp.sum(fold(jnp.where(hits(self.r, p), block, 0.0)), axis=0)
                total = total + jnp.sum(fold(powers), axis=0)
                logits[lines] = powers
            if self.top is not None:
                total = total + self.total * jnp.exp(self.top - top)
                picked = picked + self.picked
            self.top, self.total, self.picked = top, total, picked
            tops[group:group + 1] = top

        def close(self):
            total = jnp.sum(self.total, axis=0, keepdims=True)
            loss[self.r:self.r + 1] = self.top + jnp.log(total) - jnp.sum(self.picked, axis=0, keepdims=True)
            self.inverse = 1.0 / total

        def spread(self, group, part):
            factor = jnp.exp(tops[group:group + 1] - self.top) * self.inverse
            for p in SPANS[group]:
                lines = slice(128 * p, 128 * p + 128)
                share = logits[lines] * factor
                resid[lines] = jnp.where(hits(self.r, p), share - 1.0, share).astype(BF16)
            at = slice(128 * SPANS[group][0], 128 * SPANS[group][-1] + 128)
            grad = jnp.dot(resid[at], query[...], preferred_element_type=F32)
            for p in range(2 * len(SPANS[group])):
                part[SPANS[group][0] + p // 2, p % 2] = pack(grad[SHARD * p:SHARD * p + SHARD]).astype(BF16)

    def learn(r, t):
        table, totals = (src, accum) if r == 0 else (new_src, new_accum)
        grad = jnp.dot(keys_t[0:D], resid[:, tile(t)], preferred_element_type=F32) * scale[r, :, tile(t)]
        sums = totals[:, tile(t)] + jnp.sum(grad * grad, axis=0, keepdims=True) * (1.0 / D)
        new_accum[:, tile(t)] = sums
        new_src[:, tile(t)] = table[:, tile(t)] - (LEARN_RATE * grad) / jnp.sqrt(sums)

    def wide_rows(x):
        return jnp.concatenate([x, jnp.zeros((SHARD, DP - D), F32)], axis=1)

    keys0[own] = pack(wide_rows(rows[...])).astype(BF16)
    query_t[D:DP] = jnp.zeros((DP - D, SRC), BF16)
    query[:, 384:DP] = jnp.zeros((SRC, DP - 384), BF16)
    greet(me)
    gather = first_gather = Gather(keys0, *sems[0:4], me)
    gather.start()
    for t in range(3):
        relate(0, t)
        ask(0, t)
    gather.relay(0)
    gather.relay(1)
    relate(0, 3)
    ask(0, 3)
    soft = Softmax(0, keys0)

    def rest_of_gather(gather, soft):
        for col, dz in ((0, 1), (0, -1), (1, 0), (1, 1), (1, -1)):
            gather.near(col, dz)
        gather.pair(3)
        soft.score(3)
        gather.far(0, 1)
        gather.far(1, 1)
        gather.pair(2)
        soft.score(2)
        gather.far(0, 2)
        gather.far(1, 2)
        gather.pair(1)
        soft.score(1)
        gather.pair(0)
        soft.score(0)
        soft.close()

    rest_of_gather(gather, soft)

    def rest_of_scatter(scatter, soft, part, r):
        soft.spread(0, part)
        scatter.pair(0)
        soft.spread(1, part)
        scatter.pair(1)
        scatter.far(1, 2)
        scatter.far(0, 2)
        scatter.far(1, 1)
        scatter.far(0, 1)
        soft.spread(2, part)
        scatter.pair(2)
        soft.spread(3, part)
        scatter.pair(3)
        scatter.relay(1)
        scatter.relay(0)
        scatter.near(1, 1)
        scatter.near(1, -1)
        scatter.near(1, 0)
        scatter.near(0, 1)
        scatter.near(0, -1)
        for t in range(4):
            learn(r, t)

    scatter = Scatter(part0, pair0, out0, in0, *sems[4:8], me)
    rest_of_scatter(scatter, soft, part0, 0)
    grad = scatter.finish()[:, 0:D]
    updated, total = adagrad_rows(rows[...], column_of(row_accum[...]), grad)
    key_row[...] = pack(wide_rows(updated)).astype(BF16)
    shift = remote(key_row, keys1.at[own], sems[16].at[0], sems[17].at[0], beyond)
    shift.start()
    moved[...] = wide_rows(updated)
    moved[:, 384:512] = jnp.where(lax.broadcasted_iota(I32, (SHARD, 128), 1) < 16, moved[:, 384:512], total)
    carry = remote(moved, landing, sems[16].at[1], sems[17].at[1], beyond)
    carry.start()
    relate(1, 0)
    relate(1, 1)
    shift.wait_recv()
    gather = Gather(keys1, *sems[8:12], me)
    gather.start()
    relate(1, 2)
    relate(1, 3)
    ask(1, 0)
    ask(1, 1)
    gather.relay(0)
    gather.relay(1)
    ask(1, 2)
    ask(1, 3)
    soft = Softmax(1, keys1)
    rest_of_gather(gather, soft)
    scatter = Scatter(part1, pair1, out1, in1, *sems[12:16], me)
    rest_of_scatter(scatter, soft, part1, 1)
    grad = scatter.finish()[:, 0:D]
    carry.wait_recv()
    updated, total = adagrad_rows(landing[:, 0:D], landing[:, D:D + 1], grad)
    new_rows[...] = updated
    new_row_accum[...] = row_of(total)
    carry.wait_send()
    first_gather.finish()
    gather.finish()
    shift.wait_send()


VM = pl.BlockSpec(memory_space=pltpu.VMEM)
DMA = pltpu.SemaphoreType.DMA


def hand_over(*arrays):
    def kernel(*refs):
        half = len(refs) // 2
        for source, target in zip(refs[:half], refs[half:]):
            target[...] = source[...]

    return pl.pallas_call(
        kernel,
        out_shape=[jax.ShapeDtypeStruct(a.shape, a.dtype) for a in arrays],
        in_specs=[VM] * len(arrays),
        out_specs=[VM] * len(arrays),
    )(*arrays)


def shards(src_rows, src_accum, dst_rows, dst_accum, relations, rel_ids, targets):
    twice = lambda shape, kind: [pltpu.VMEM(shape, kind)] * 2
    new_src, new_accum, new_rows, new_row_accum, loss = pl.pallas_call(
        train_kernel,
        out_shape=[
            jax.ShapeDtypeStruct(s, F32) for s in ((D, SRC), (1, SRC), (SHARD, D), (1, SHARD), (2, SRC))
        ],
        in_specs=[VM] * 7,
        out_specs=[VM] * 5,
        scratch_shapes=[
            pltpu.VMEM((2, D, SRC), F32), pltpu.VMEM((DP, SRC), BF16), pltpu.VMEM((SRC, DP), BF16),
            pltpu.VMEM((BUCKET, SRC), F32), pltpu.VMEM((BUCKET, SRC), BF16), pltpu.VMEM((DP, BUCKET), BF16),
            *twice((32, SLOT, 128), BF16), *twice((CHIPS, 2, SLOT, 128), BF16), *twice((CHIPS, SLOT, 128), BF16),
            *twice((STEPS, SLOT, 128), BF16), *twice((STEPS, SLOT, 128), BF16),
            pltpu.VMEM((SLOT, 128), BF16), *twice((SHARD, DP), F32), pltpu.VMEM((8, SRC), F32),
            *([DMA((STEPS,)), DMA((STEPS,)), DMA((CHIPS,)), DMA((CHIPS,))] * 4), DMA((2,)), DMA((2,)),
        ],
        compiler_params=pltpu.CompilerParams(
            collective_id=0, has_side_effects=True, vmem_limit_bytes=62 * 1024 * 1024,
        ),
    )(src_rows.T, src_accum.reshape(1, SRC), dst_rows, dst_accum.reshape(1, SHARD), relations.T, rel_ids, targets)
    (new_src, new_accum, new_rows, new_row_accum, loss) = hand_over(new_src, new_accum, new_rows, new_row_accum, loss)
    return (new_src.T, new_accum.reshape(SRC), new_rows, new_row_accum.reshape(SHARD), loss)


def solution(mesh):
    both = ("grp", "wide")
    placed = (P(both, None), P(both), P(both, None), P(both), P(), P(None, both), P(None, both))
    return jax.shard_map(
        shards, mesh=mesh, in_specs=placed,
        out_specs=(P(both, None), P(both), P(both, None), P(both), P(None, both)),
        check_vma=False,
    )
```

time: 115 us -> 90.6 us (0.79)
  Pallas kernels: 108 us -> 89.1 us
  local copies, waits for them, and re-layouts: 5.21 us -> 0 us
    pallas_call x1, Pallas kernels: 108 us -> 86.3 us  [shards(): pl.pallas_call(train_kernel, out_shape=[jax.ShapeDtypeStruct(s, F32) for...]
    unnamed x13 -> x0, local copies, waits for them, and re-layouts: 5.21 us -> none
    pallas_call x0 -> x1, Pallas kernels: none -> 2.75 us  [hand_over(): pl.pallas_call(kernel, out_shape=[jax.ShapeDtypeStruct(a.shape, a.dtype)...]
where the time goes in v3:
time: 90.6 us; the launch traced here: 89.7 us
  Pallas kernels  89.1 us (98%)
    pallas_call x1, Pallas kernels, shards(): pl.pallas_call(train_kernel, out_shape=[jax.ShapeDtypeStruct(s, F32) for...  86.3 us
    pallas_call x1, Pallas kernels, hand_over(): pl.pallas_call(kernel, out_shape=[jax.ShapeDtypeStruct(a.shape, a.dtype)...  2.75 us

profile of v3, /device:TPU:32, one launch (start us, length us, event | category | flops | bytes accessed | tf_op | source)
XLA Modules:
  0.0 89.7 jit_solution(13547938981536529181)
XLA Ops:
  0.6 86.3 %shard_map.110 = (f32[400,1024]{1,0:T(8,128)}, f32[1,1024]{1,0:T(1,128)}, f32[64,400]{1,0:T(8,128)}, f32[1,64]{1,0:T(1,128)}, f32[2,1024]{1,0:T(2,128)}) custom-call(f32[400,1024]{1,0:T(8,128)} %bitcast.7, f32[1,1024]{1,0:T(1,128)} %bitcast.9, f32[64,400]{1,0:T(8,128)} %rows.1, f32[1,64]{1,0:T(1,128)} %bitcast.10, f32[400,1024]{1,0:T(8,128)} %bitcast.8, ...), custom_call_target="tpu_custom_call" | custom-call | tf_op jit(solution)/shard_map/pallas_call | solution.py:447
  87.0 2.7 %shard_map.111 = (f32[400,1024]{1,0:T(8,128)}, f32[1,1024]{1,0:T(1,128)}, f32[64,400]{1,0:T(8,128)}, f32[1,64]{1,0:T(1,128)}, f32[2,1024]{1,0:T(2,128)}) custom-call(f32[400,1024]{1,0:T(8,128)} %get-tuple-element.15.refs_0_, f32[1,1024]{1,0:T(1,128)} %get-tuple-element.16.refs_1_, f32[64,400]{1,0:T(8,128)} %get-tuple-element.17.refs_2_, ...), custom_call_target="tpu_custom_call" | custom-call | tf_op jit(solution)/shard_map/pallas_call | solution.py:437

commit v4 on v3

--- a/solution.py
+++ b/solution.py
@@ -14,14 +14,14 @@
 GROUPS = (
     ((1, 4), (0, 4)),
     ((1, 3), (1, -3), (0, 3), (0, -3)),
-    ((1, 2), (1, -2), (0, 2), (0, -2)),
-    ((0, 1), (0, -1), (1, 0), (0, 0), (1, 1), (1, -1)),
+    ((0, 1), (0, -1), (1, 1), (1, -1)),
+    ((1, 2), (1, -2), (0, 2), (0, -2), (1, 0), (0, 0)),
 )
 BLOCKS = sum(GROUPS, ())
 SPOT = {(col, dz % NZ): p for p, (col, dz) in enumerate(BLOCKS)}
 SPANS = tuple(range(sum(map(len, GROUPS[:n])), sum(map(len, GROUPS[:n + 1]))) for n in range(len(GROUPS)))
 SLOT = 208
-DIRECT = ((0, 2), (0, -2), (1, 2), (1, -2), (0, 1), (0, -1), (1, 0), (1, 1), (1, -1))
+DIRECT = ((1, 2), (1, -2), (0, 2), (0, -2), (1, 0), (1, 1), (1, -1), (0, 1), (0, -1))
 RELAYS = tuple((col, way, more) for col in (0, 1) for way in (1, -1) for more in (1, 2) if more == 1 or way == (1, -1)[col])
 STEPS = len(DIRECT) + len(RELAYS) + 1
 HOME = STEPS - 1
@@ -236,7 +236,7 @@
 
 def train_kernel(src, accum, rows, row_accum, rels, ids, labels,
                  new_src, new_accum, new_rows, new_row_accum, loss,
-                 scale, query_t, query, logits, resid, keys_t,
+                 scale, query_t, query, logits, resid, keys_t, key_rows,
                  keys0, keys1, part0, part1, pair0, pair1, out0, out1, in0, in1, key_row, moved, landing, tops,
                  *sems):
     me = g, y, z, core = place()
@@ -263,18 +263,18 @@
         query_t[0:D, tile(t)] = quarter
         query[tile(t), 0:D] = quarter.T
 
-    def hits(r, p):
+    def hits(r, p, t):
         col, dz = BLOCKS[p]
         chip = (y if col == 0 else 1 - y) * NZ + wrap(z + dz)
-        return lax.broadcasted_iota(I32, (128, SRC), 0) == labels[r:r + 1, :] - 128 * chip
+        return lax.broadcasted_iota(I32, (128, 256), 0) == labels[r:r + 1, tile(t)] - 128 * chip
 
     def fold(x):
-        return x.reshape(-1, 8, SRC)
+        return x.reshape(-1, 8, x.shape[1])
 
     class Softmax:
         def __init__(self, r, keys):
-            self.r, self.keys, self.top = r, keys, None
-            self.total = self.picked = None
+            self.r, self.keys = r, keys
+            self.top, self.total, self.picked = [None] * 4, [None] * 4, [None] * 4
 
         def score(self, group):
             pieces = []
@@ -283,36 +283,49 @@
                 pieces.append(jnp.concatenate([self.keys[s, 0:64], self.keys[s, 64:128], self.keys[s, 128:192], end], axis=1))
             rows_ = jnp.concatenate(pieces, axis=0)
             at = slice(128 * SPANS[group][0], 128 * SPANS[group][-1] + 128)
-            keys_t[:, at] = rows_.T
-            logits[at] = jnp.dot(rows_, query_t[...], preferred_element_type=F32)
-            top = jnp.max(jnp.max(fold(logits[at]), axis=0), axis=0, keepdims=True)
-            if self.top is not None:
-                top = jnp.maximum(top, self.top)
-            total = picked = jnp.zeros((8, SRC), F32)
+            key_rows[at] = rows_
+            for t in range(4):
+                self.weigh(group, at, rows_, t)
+
+        def weigh(self, group, at, rows_, t):
+            block = jnp.dot(rows_, query_t[:, tile(t)], preferred_element_type=F32)
+            logits[at, tile(t)] = block
+            top = jnp.max(jnp.max(fold(block), axis=0), axis=0, keepdims=True)
+            if self.top[t] is not None:
+                top = jnp.maximum(top, self.top[t])
+            total = picked = jnp.zeros((8, 256), F32)
             for p in SPANS[group]:
                 lines = slice(128 * p, 128 * p + 128)
-                block = logits[lines]
+                block = logits[lines, tile(t)]
                 powers = jnp.exp(block - top)
-                picked = picked + jnp.sum(fold(jnp.where(hits(self.r, p), block, 0.0)), axis=0)
+                picked = picked + jnp.sum(fold(jnp.where(hits(self.r, p, t), block, 0.0)), axis=0)
                 total = total + jnp.sum(fold(powers), axis=0)
-                logits[lines] = powers
-            if self.top is not None:
-                total = total + self.total * jnp.exp(self.top - top)
-                picked = picked + self.picked
-            self.top, self.total, self.picked = top, total, picked
-            tops[group:group + 1] = top
+                logits[lines, tile(t)] = powers
+            if self.top[t] is not None:
+                total = total + self.total[t] * jnp.exp(self.top[t] - top)
+                picked = picked + self.picked[t]
+            self.top[t], self.total[t], self.picked[t] = top, total, picked
+            tops[group:group + 1, tile(t)] = top
+
+        def flip(self, group):
+            at = slice(128 * SPANS[group][0], 128 * SPANS[group][-1] + 128)
+            keys_t[:, at] = key_rows[at].T
 
         def close(self):
-            total = jnp.sum(self.total, axis=0, keepdims=True)
-            loss[self.r:self.r + 1] = self.top + jnp.log(total) - jnp.sum(self.picked, axis=0, keepdims=True)
-            self.inverse = 1.0 / total
+            self.inverse = []
+            for t in range(4):
+                total = jnp.sum(self.total[t], axis=0, keepdims=True)
+                picked = jnp.sum(self.picked[t], axis=0, keepdims=True)
+                loss[self.r:self.r + 1, tile(t)] = self.top[t] + jnp.log(total) - picked
+                self.inverse.append(1.0 / total)
 
         def spread(self, group, part):
-            factor = jnp.exp(tops[group:group + 1] - self.top) * self.inverse
-            for p in SPANS[group]:
-                lines = slice(128 * p, 128 * p + 128)
-                share = logits[lines] * factor
-                resid[lines] = jnp.where(hits(self.r, p), share - 1.0, share).astype(BF16)
+            for t in range(4):
+                factor = jnp.exp(tops[group:group + 1, tile(t)] - self.top[t]) * self.inverse[t]
+                for p in SPANS[group]:
+                    lines = slice(128 * p, 128 * p + 128)
+                    share = logits[lines, tile(t)] * factor
+                    resid[lines, tile(t)] = jnp.where(hits(self.r, p, t), share - 1.0, share).astype(BF16)
             at = slice(128 * SPANS[group][0], 128 * SPANS[group][-1] + 128)
             grad = jnp.dot(resid[at], query[...], preferred_element_type=F32)
             for p in range(2 * len(SPANS[group])):
@@ -344,10 +357,11 @@
     soft = Softmax(0, keys0)
 
     def rest_of_gather(gather, soft):
-        for col, dz in ((0, 1), (0, -1), (1, 0), (1, 1), (1, -1)):
-            gather.near(col, dz)
+        gather.near(1, 0)
         gather.pair(3)
         soft.score(3)
+        for col, dz in ((1, 1), (1, -1), (0, 1), (0, -1)):
+            gather.near(col, dz)
         gather.far(0, 1)
         gather.far(1, 1)
         gather.pair(2)
@@ -375,13 +389,13 @@
         scatter.pair(2)
         soft.spread(3, part)
         scatter.pair(3)
+        for col, dz in ((1, 1), (1, -1), (0, 1), (0, -1)):
+            scatter.near(col, dz)
         scatter.relay(1)
+        scatter.near(1, 0)
         scatter.relay(0)
-        scatter.near(1, 1)
-        scatter.near(1, -1)
-        scatter.near(1, 0)
-        scatter.near(0, 1)
-        scatter.near(0, -1)
+        for group in range(4):
+            soft.flip(group)
         for t in range(4):
             learn(r, t)
 
@@ -454,6 +468,7 @@
         scratch_shapes=[
             pltpu.VMEM((2, D, SRC), F32), pltpu.VMEM((DP, SRC), BF16), pltpu.VMEM((SRC, DP), BF16),
             pltpu.VMEM((BUCKET, SRC), F32), pltpu.VMEM((BUCKET, SRC), BF16), pltpu.VMEM((DP, BUCKET), BF16),
+            pltpu.VMEM((BUCKET, DP), BF16),
             *twice((32, SLOT, 128), BF16), *twice((CHIPS, 2, SLOT, 128), BF16), *twice((CHIPS, SLOT, 128), BF16),
             *twice((STEPS, SLOT, 128), BF16), *twice((STEPS, SLOT, 128), BF16),
             pltpu.VMEM((SLOT, 128), BF16), *twice((SHARD, DP), F32), pltpu.VMEM((8, SRC), F32),

time: 90.6 us -> 89.4 us (0.987)
  Pallas kernels: 89.1 us -> 87.9 us
    pallas_call x1, Pallas kernels: 86.3 us -> 85.2 us  [shards(): pl.pallas_call(train_kernel, out_shape=[jax.ShapeDtypeStruct(s, F32) for...]
where the time goes in v4:
time: 89.4 us; the launch traced here: 88.5 us
  Pallas kernels  87.9 us (98%)
    pallas_call x1, Pallas kernels, shards(): pl.pallas_call(train_kernel, out_shape=[jax.ShapeDtypeStruct(s, F32) for...  85.2 us
    pallas_call x1, Pallas kernels, hand_over(): pl.pallas_call(kernel, out_shape=[jax.ShapeDtypeStruct(a.shape, a.dtype)...  2.75 us

profile of v4, /device:TPU:32, one launch (start us, length us, event | category | flops | bytes accessed | tf_op | source)
XLA Modules:
  0.0 88.5 jit_solution(2636119752530358610)
XLA Ops:
  0.6 85.2 %shard_map.110 = (f32[400,1024]{1,0:T(8,128)}, f32[1,1024]{1,0:T(1,128)}, f32[64,400]{1,0:T(8,128)}, f32[1,64]{1,0:T(1,128)}, f32[2,1024]{1,0:T(2,128)}) custom-call(f32[400,1024]{1,0:T(8,128)} %bitcast.7, f32[1,1024]{1,0:T(1,128)} %bitcast.9, f32[64,400]{1,0:T(8,128)} %rows.1, f32[1,64]{1,0:T(1,128)} %bitcast.10, f32[400,1024]{1,0:T(8,128)} %bitcast.8, ...), custom_call_target="tpu_custom_call" | custom-call | tf_op jit(solution)/shard_map/pallas_call | solution.py:461
  85.8 2.7 %shard_map.111 = (f32[400,1024]{1,0:T(8,128)}, f32[1,1024]{1,0:T(1,128)}, f32[64,400]{1,0:T(8,128)}, f32[1,64]{1,0:T(1,128)}, f32[2,1024]{1,0:T(2,128)}) custom-call(f32[400,1024]{1,0:T(8,128)} %get-tuple-element.15.refs_0_, f32[1,1024]{1,0:T(1,128)} %get-tuple-element.16.refs_1_, f32[64,400]{1,0:T(8,128)} %get-tuple-element.17.refs_2_, ...), custom_call_target="tpu_custom_call" | custom-call | tf_op jit(solution)/shard_map/pallas_call | solution.py:451

commit v5 on v4

--- a/solution.py
+++ b/solution.py
@@ -389,11 +389,13 @@
         scatter.pair(2)
         soft.spread(3, part)
         scatter.pair(3)
-        for col, dz in ((1, 1), (1, -1), (0, 1), (0, -1)):
-            scatter.near(col, dz)
+        scatter.near(1, 1)
+        scatter.near(1, -1)
         scatter.relay(1)
+        scatter.relay(0)
+        scatter.near(0, 1)
+        scatter.near(0, -1)
         scatter.near(1, 0)
-        scatter.relay(0)
         for group in range(4):
             soft.flip(group)
         for t in range(4):

time: 89.4 us -> 87 us (0.973)
  Pallas kernels: 87.9 us -> 84.8 us
    pallas_call x1, Pallas kernels: 85.2 us -> 82.1 us  [shards(): pl.pallas_call(train_kernel, out_shape=[jax.ShapeDtypeStruct(s, F32) for...]
where the time goes in v5:
time: 87 us; the launch traced here: 85.5 us
  Pallas kernels  84.8 us (97%)
    pallas_call x1, Pallas kernels, shards(): pl.pallas_call(train_kernel, out_shape=[jax.ShapeDtypeStruct(s, F32) for...  82.1 us
    pallas_call x1, Pallas kernels, hand_over(): pl.pallas_call(kernel, out_shape=[jax.ShapeDtypeStruct(a.shape, a.dtype)...  2.75 us

profile of v5, /device:TPU:32, one launch (start us, length us, event | category | flops | bytes accessed | tf_op | source)
XLA Modules:
  0.0 85.5 jit_solution(2564249330338765335)
XLA Ops:
  0.6 82.1 %shard_map.110 = (f32[400,1024]{1,0:T(8,128)}, f32[1,1024]{1,0:T(1,128)}, f32[64,400]{1,0:T(8,128)}, f32[1,64]{1,0:T(1,128)}, f32[2,1024]{1,0:T(2,128)}) custom-call(f32[400,1024]{1,0:T(8,128)} %bitcast.7, f32[1,1024]{1,0:T(1,128)} %bitcast.9, f32[64,400]{1,0:T(8,128)} %rows.1, f32[1,64]{1,0:T(1,128)} %bitcast.10, f32[400,1024]{1,0:T(8,128)} %bitcast.8, ...), custom_call_target="tpu_custom_call" | custom-call | tf_op jit(solution)/shard_map/pallas_call | solution.py:463
  82.7 2.7 %shard_map.111 = (f32[400,1024]{1,0:T(8,128)}, f32[1,1024]{1,0:T(1,128)}, f32[64,400]{1,0:T(8,128)}, f32[1,64]{1,0:T(1,128)}, f32[2,1024]{1,0:T(2,128)}) custom-call(f32[400,1024]{1,0:T(8,128)} %get-tuple-element.15.refs_0_, f32[1,1024]{1,0:T(1,128)} %get-tuple-element.16.refs_1_, f32[64,400]{1,0:T(8,128)} %get-tuple-element.17.refs_2_, ...), custom_call_target="tpu_custom_call" | custom-call | tf_op jit(solution)/shard_map/pallas_call | solution.py:453

commit v6 on v5

--- a/solution.py
+++ b/solution.py
@@ -450,11 +450,14 @@
         for source, target in zip(refs[:half], refs[half:]):
             target[...] = source[...]
 
+    blocks = [pl.BlockSpec((D, SRC // 4), lambda t: (0, t))]
+    blocks += [pl.BlockSpec(a.shape, lambda t: (0, 0)) for a in arrays[1:]]
     return pl.pallas_call(
         kernel,
         out_shape=[jax.ShapeDtypeStruct(a.shape, a.dtype) for a in arrays],
-        in_specs=[VM] * len(arrays),
-        out_specs=[VM] * len(arrays),
+        grid=(4,),
+        in_specs=blocks,
+        out_specs=blocks,
     )(*arrays)
 
 

time: 87 us -> 88.2 us (1.014)
  Pallas kernels: 84.8 us -> 85.8 us
    pallas_call x1, Pallas kernels: 2.75 us -> 3.72 us  [hand_over(): pl.pallas_call(kernel, out_shape=[jax.ShapeDtypeStruct(a.shape, a.dtype)...]
where the time goes in v6:
time: 88.2 us; the launch traced here: 86.6 us
  Pallas kernels  85.8 us (97%)
    pallas_call x1, Pallas kernels, shards(): pl.pallas_call(train_kernel, out_shape=[jax.ShapeDtypeStruct(s, F32) for...  82.1 us
    pallas_call x1, Pallas kernels, hand_over(): pl.pallas_call(kernel, out_shape=[jax.ShapeDtypeStruct(a.shape, a.dtype)...  3.72 us

profile of v6, /device:TPU:32, one launch (start us, length us, event | category | flops | bytes accessed | tf_op | source)
XLA Modules:
  0.0 86.6 jit_solution(10700264402636777321)
XLA Ops:
  0.6 82.1 %shard_map.110 = (f32[400,1024]{1,0:T(8,128)}, f32[1,1024]{1,0:T(1,128)}, f32[64,400]{1,0:T(8,128)}, f32[1,64]{1,0:T(1,128)}, f32[2,1024]{1,0:T(2,128)}) custom-call(f32[400,1024]{1,0:T(8,128)} %bitcast.7, f32[1,1024]{1,0:T(1,128)} %bitcast.9, f32[64,400]{1,0:T(8,128)} %rows.1, f32[1,64]{1,0:T(1,128)} %bitcast.10, f32[400,1024]{1,0:T(8,128)} %bitcast.8, ...), custom_call_target="tpu_custom_call" | custom-call | tf_op jit(solution)/shard_map/pallas_call | solution.py:466
  82.7 3.7 %shard_map.111 = (f32[400,1024]{1,0:T(8,128)}, f32[1,1024]{1,0:T(1,128)}, f32[64,400]{1,0:T(8,128)}, f32[1,64]{1,0:T(1,128)}, f32[2,1024]{1,0:T(2,128)}) custom-call(f32[400,1024]{1,0:T(8,128)} %get-tuple-element.15.refs_0_, f32[1,1024]{1,0:T(1,128)} %get-tuple-element.16.refs_1_, f32[64,400]{1,0:T(8,128)} %get-tuple-element.17.refs_2_, ...), custom_call_target="tpu_custom_call" | custom-call | tf_op jit(solution)/shard_map/pallas_call | solution.py:455
